TPU v7x, 256 devices: a whole 4x4x8 slice. The times are simulated.
256 devices in a mesh: dp: 2 (over z_hi), context: 8 (over y, core), tensor: 16 (over z_lo, x).
Axes of the slice: x: 4, y: 4, z: 8 (z_hi: 2, z_lo: 4; z = z_hi * 4 + z_lo), core: 2. Of those that a mesh axis runs over, the one named last changes fastest.
Arguments:
- tokens: bfloat16 [2, 4096, 5376], P('dp', ('context', 'tensor')), may hold values from -48 to 48
- output_gradient: bfloat16 [2, 4096, 5376], P('dp', ('context', 'tensor')), may hold values from -48 to 48
- document_index: int32 [2, 4096], P('dp'), may hold values from 0 to 3, never falling along the last dimension, each value on 1 to 2048 neighbouring positions
- query_weight: bfloat16 [5376, 4096], P(None, 'tensor'), may hold values from -1 to 1
- key_value_weight: bfloat16 [2, 5376, 2048], P(None, None, 'tensor'), may hold values from -1 to 1
- output_weight: bfloat16 [4096, 5376], P('tensor'), may hold values from -0.09375 to 0.09375
- adapter_down_projections: bfloat16 [3, 16, 5376], replicated, may hold values from -0.078125 to 0.078125
- adapter_up_query: bfloat16 [16, 4096], P(None, 'tensor'), may hold values from -0.29882812 to 0.29882812
- adapter_up_key_value: bfloat16 [2, 16, 2048], P(None, None, 'tensor'), may hold values from -0.29882812 to 0.29882812
- adapter_down_output: bfloat16 [16, 4096], P(None, 'tensor'), may hold values from -0.09375 to 0.09375
- adapter_up_output: bfloat16 [16, 5376], replicated, may hold values from -0.29882812 to 0.29882812
Outputs:
- grad_input: bfloat16 [2, 4096, 5376], P('dp', ('context', 'tensor'))
- grad_down_qkv: float32 [3, 16, 5376], replicated
- query_up_gradient: float32 [16, 4096], P(None, 'tensor')
- grad_up_keyvalue: float32 [2, 16, 2048], P(None, None, 'tensor')
- grad_down_out: float32 [16, 4096], P(None, 'tensor')
- output_up_gradient: float32 [16, 5376], replicated
Inputs may be any that keep to these rules, and one draw needn't show every extreme that they name: `document_index`: ids never fall along a sequence; each document holds 1 to half of 4096 tokens, and one holds exactly that many.
All inputs are finite; a program needn't handle non-finite values.
Results may differ from a plain program's by a relative error of at most 0.03.
Values may be sent and summed in bfloat16 or wider, within the bound.
No kernel may reach another device: no remote copies, remote signals or barrier semaphores. Data moves between devices by JAX's collectives and lax.ppermute only.
A program may use at most 128 MiB of HBM per device.

v0:
```python
import jax
import jax.numpy as jnp
from jax import lax
from jax.sharding import PartitionSpec as P

HEAD_SIZE = 128
WINDOW = 1024
adapter_scale = 2.0
attn_scale = 168.0 ** (-0.5)
rope_base = 10000.0


def passed_along(block, axis, distance):
    devices = range(lax.axis_size(axis))
    route = [(i - distance, i) for i in devices if i - distance in devices]
    return lax.ppermute(block, axis, route)


def rope_tables(positions, head_width):
    half_width = head_width // 2
    inverse = rope_base ** (-(jnp.arange(half_width, dtype=jnp.float32) * 2.0 / head_width))
    angle = positions[:, None] * inverse[None, :]
    return (jnp.cos(angle), jnp.sin(angle))


def apply_rotation(vectors, cosine_table, sine_values):
    half_width = vectors.shape[-1] // 2
    front_half = vectors[..., :half_width]
    back_half = vectors[..., half_width:]
    cosine_table = cosine_table[:, None, :]
    sine_values = sine_values[:, None, :]
    return jnp.concatenate(
        [
            front_half * cosine_table - back_half * sine_values,
            back_half * cosine_table + front_half * sine_values,
        ],
        -1,
    )


def undo_rotation(grads, cosine_table, sine_values):
    half_width = grads.shape[-1] // 2
    front_half = grads[..., :half_width]
    back_half = grads[..., half_width:]
    cosine_table = cosine_table[:, None, :]
    sine_values = sine_values[:, None, :]
    return jnp.concatenate(
        [
            front_half * cosine_table + back_half * sine_values,
            back_half * cosine_table - front_half * sine_values,
        ],
        -1,
    )


def band_block(queries, key_rows, value_rows, attention_output_gradient, allowed):
    row_count, heads_q, head_width = queries.shape
    heads_kv = key_rows.shape[1]
    group_size = heads_q // heads_kv
    query_groups = queries.reshape(row_count, heads_kv, group_size, head_width)
    grad_groups = attention_output_gradient.reshape(row_count, heads_kv, group_size, head_width)
    scores = (
        jnp.einsum("chgd,khd->hgck", query_groups, key_rows, preferred_element_type=jnp.float32)
        * attn_scale
    )
    scores = jnp.where(allowed[None, None], scores, -1e30)
    row_max = jnp.max(scores, -1, keepdims=True)
    exponent = jnp.exp(scores - row_max)
    weights = exponent / jnp.sum(exponent, -1, keepdims=True)
    weights_low = weights.astype(jnp.bfloat16)
    attention_output = jnp.einsum(
        "hgck,khd->chgd", weights_low, value_rows, preferred_element_type=jnp.float32
    ).astype(jnp.bfloat16)
    grad_weights = jnp.einsum(
        "chgd,khd->hgck", grad_groups, value_rows, preferred_element_type=jnp.float32
    )
    row_dot = jnp.einsum(
        "chgd,chgd->hgc", grad_groups.astype(jnp.float32), attention_output.astype(jnp.float32)
    )
    grad_scores = (weights * (grad_weights - row_dot[..., None]) * attn_scale).astype(jnp.bfloat16)
    query_gradient = jnp.einsum(
        "hgck,khd->chgd", grad_scores, key_rows, preferred_element_type=jnp.float32
    )
    key_gradient = jnp.einsum(
        "hgck,chgd->khd", grad_scores, query_groups, preferred_element_type=jnp.float32
    )
    value_gradient = jnp.einsum(
        "hgck,chgd->khd", weights_low, grad_groups, preferred_element_type=jnp.float32
    )
    return (
        attention_output.reshape(row_count, heads_q, head_width),
        query_gradient.reshape(row_count, heads_q, head_width),
        key_gradient,
        value_gradient,
    )


def local(
    tokens,
    output_gradient,
    document_index,
    query_weight,
    key_value_weight,
    output_weight,
    adapter_down_projections,
    adapter_up_query,
    adapter_up_key_value,
    adapter_down_output,
    adapter_up_output,
):
    tensor_size = lax.axis_size("tensor")
    context_at = lax.axis_index("context")
    local_count = tokens.shape[1]
    model_width_size = tokens.shape[2]
    shard_len = local_count * tensor_size
    halo_count = (WINDOW - 1) // shard_len + 1
    rank_width_size = adapter_down_projections.shape[1]
    heads_q = query_weight.shape[1] // HEAD_SIZE
    heads_kv = key_value_weight.shape[2] // HEAD_SIZE
    gathered, incoming_gradient = (
        lax.all_gather(tokens[0], "tensor", axis=0, tiled=True),
        lax.all_gather(output_gradient[0], "tensor", axis=0, tiled=True),
    )
    down_factors_all = adapter_down_projections.reshape(3 * rank_width_size, model_width_size)
    adapted = jnp.einsum(
        "ja,ma->jm", gathered, down_factors_all, preferred_element_type=jnp.float32
    ).astype(jnp.bfloat16)
    adapted_query = adapted[:, :rank_width_size]
    adapted_key = adapted[:, rank_width_size : 2 * rank_width_size]
    adapted_value = adapted[:, 2 * rank_width_size :]
    query_linear = jnp.dot(
        gathered, query_weight, preferred_element_type=jnp.float32
    ) + adapter_scale * jnp.dot(adapted_query, adapter_up_query, preferred_element_type=jnp.float32)
    key_linear = jnp.dot(
        gathered, key_value_weight[0], preferred_element_type=jnp.float32
    ) + adapter_scale * jnp.dot(
        adapted_key, adapter_up_key_value[0], preferred_element_type=jnp.float32
    )
    value_linear = jnp.dot(
        gathered, key_value_weight[1], preferred_element_type=jnp.float32
    ) + adapter_scale * jnp.dot(
        adapted_value, adapter_up_key_value[1], preferred_element_type=jnp.float32
    )
    positions = (context_at * shard_len + jnp.arange(shard_len, dtype=jnp.int32)).astype(
        jnp.float32
    )
    cosine_table, sine_values = rope_tables(positions, HEAD_SIZE)
    queries = apply_rotation(
        query_linear.reshape(shard_len, heads_q, HEAD_SIZE), cosine_table, sine_values
    ).astype(jnp.bfloat16)
    key_local = apply_rotation(
        key_linear.reshape(shard_len, heads_kv, HEAD_SIZE), cosine_table, sine_values
    ).astype(jnp.bfloat16)
    value_local = value_linear.reshape(shard_len, heads_kv, HEAD_SIZE).astype(jnp.bfloat16)
    pair_local = jnp.stack([key_local, value_local], 0)
    earlier = [
        passed_along(pair_local, "context", distance) for distance in range(halo_count, 0, -1)
    ]
    pairs = jnp.concatenate(earlier + [pair_local], 1)
    segment_row = document_index[0]
    segment_pad = jnp.concatenate(
        [jnp.full((halo_count * shard_len,), -1, jnp.int32), segment_row], 0
    )
    key_seg = lax.dynamic_slice_in_dim(
        segment_pad, context_at * shard_len, (halo_count + 1) * shard_len, 0
    )
    query_seg = lax.dynamic_slice_in_dim(segment_row, context_at * shard_len, shard_len, 0)
    query_pos = context_at * shard_len + jnp.arange(shard_len, dtype=jnp.int32)
    key_pos = (context_at - halo_count) * shard_len + jnp.arange(
        (halo_count + 1) * shard_len, dtype=jnp.int32
    )
    offset = query_pos[:, None] - key_pos[None, :]
    allowed = (
        (key_pos >= 0)[None, :]
        & (offset >= 0)
        & (offset < WINDOW)
        & (query_seg[:, None] == key_seg[None, :])
    )
    up_gradient = (
        adapter_scale
        * jnp.einsum(
            "ja,ma->jm", incoming_gradient, adapter_up_output, preferred_element_type=jnp.float32
        )
    ).astype(jnp.bfloat16)
    attention_output_gradient = (
        jnp.einsum(
            "td,hd->th", incoming_gradient, output_weight, preferred_element_type=jnp.float32
        )
        + jnp.dot(up_gradient, adapter_down_output, preferred_element_type=jnp.float32)
    ).astype(jnp.bfloat16)
    attention_output, grad_query_rot, grad_keys_all, grad_values_all = band_block(
        queries,
        pairs[0],
        pairs[1],
        attention_output_gradient.reshape(shard_len, heads_q, HEAD_SIZE),
        allowed,
    )
    grad_pairs = jnp.stack([grad_keys_all, grad_values_all], 0)

    def share_for(distance):
        return lax.slice_in_dim(
            grad_pairs,
            (halo_count - distance) * shard_len,
            (halo_count - distance + 1) * shard_len,
            axis=1,
        )

    combined = share_for(0)
    for distance in range(1, halo_count + 1):
        combined = combined + passed_along(
            share_for(distance).astype(jnp.bfloat16), "context", -distance
        ).astype(jnp.float32)
    attention_output_flat = attention_output.reshape(shard_len, heads_q * HEAD_SIZE)
    query_gradient = (
        undo_rotation(grad_query_rot, cosine_table, sine_values)
        .reshape(shard_len, heads_q * HEAD_SIZE)
        .astype(jnp.bfloat16)
    )
    key_gradient = (
        undo_rotation(combined[0], cosine_table, sine_values)
        .reshape(shard_len, heads_kv * HEAD_SIZE)
        .astype(jnp.bfloat16)
    )
    value_gradient = combined[1].reshape(shard_len, heads_kv * HEAD_SIZE).astype(jnp.bfloat16)
    query_hidden = (
        adapter_scale
        * jnp.einsum(
            "kn,pn->kp", query_gradient, adapter_up_query, preferred_element_type=jnp.float32
        )
    ).astype(jnp.bfloat16)
    key_hidden = (
        adapter_scale
        * jnp.einsum(
            "kn,pn->kp", key_gradient, adapter_up_key_value[0], preferred_element_type=jnp.float32
        )
    ).astype(jnp.bfloat16)
    value_hidden = (
        adapter_scale
        * jnp.einsum(
            "kn,pn->kp", value_gradient, adapter_up_key_value[1], preferred_element_type=jnp.float32
        )
    ).astype(jnp.bfloat16)
    hidden_all = jnp.concatenate([query_hidden, key_hidden, value_hidden], 1)
    grad_down_part = jnp.einsum(
        "tr,td->rd", hidden_all, gathered, preferred_element_type=jnp.float32
    ).reshape(3, rank_width_size, model_width_size)
    query_up_gradient_piece = adapter_scale * jnp.einsum(
        "tr,th->rh", adapted_query, query_gradient, preferred_element_type=jnp.float32
    )
    grad_up_kv_part = jnp.stack(
        [
            adapter_scale
            * jnp.einsum(
                "tr,th->rh", adapted_key, key_gradient, preferred_element_type=jnp.float32
            ),
            adapter_scale
            * jnp.einsum(
                "tr,th->rh", adapted_value, value_gradient, preferred_element_type=jnp.float32
            ),
        ],
        0,
    )
    grad_down_out_part = jnp.einsum(
        "tr,th->rh", up_gradient, attention_output_flat, preferred_element_type=jnp.float32
    )
    factor_part = jnp.einsum(
        "kn,pn->kp", attention_output_flat, adapter_down_output, preferred_element_type=jnp.float32
    )
    factor_value = lax.psum(factor_part.astype(jnp.bfloat16), "tensor")
    output_up_gradient_piece = adapter_scale * jnp.einsum(
        "tr,td->rd", factor_value, incoming_gradient, preferred_element_type=jnp.float32
    )
    grad_down_qkv = lax.psum(grad_down_part, ("dp", "context", "tensor"))
    query_up_gradient, grad_up_keyvalue, grad_down_out, output_up_gradient = (
        lax.psum(query_up_gradient_piece.astype(jnp.bfloat16), ("dp", "context")).astype(
            jnp.float32
        ),
        lax.psum(grad_up_kv_part.astype(jnp.bfloat16), ("dp", "context")).astype(jnp.float32),
        lax.psum(grad_down_out_part.astype(jnp.bfloat16), ("dp", "context")).astype(jnp.float32),
        lax.psum(output_up_gradient_piece.astype(jnp.bfloat16), ("dp", "context")).astype(
            jnp.float32
        ),
    )
    term = jnp.einsum("th,dh->td", query_gradient, query_weight, preferred_element_type=jnp.float32)
    term = term + jnp.einsum(
        "th,dh->td", key_gradient, key_value_weight[0], preferred_element_type=jnp.float32
    )
    term = term + jnp.einsum(
        "th,dh->td", value_gradient, key_value_weight[1], preferred_element_type=jnp.float32
    )
    full_sum = lax.psum(
        (term + jnp.dot(hidden_all, down_factors_all, preferred_element_type=jnp.float32)).astype(
            jnp.bfloat16
        ),
        "tensor",
    ).astype(jnp.float32)
    mine = lax.dynamic_slice_in_dim(
        full_sum, lax.axis_index("tensor") * local_count, local_count, 0
    )
    grad_input = mine.astype(jnp.bfloat16)[None]
    return (
        grad_input,
        grad_down_qkv,
        query_up_gradient,
        grad_up_keyvalue,
        grad_down_out,
        output_up_gradient,
    )


def solution(mesh):
    in_specs = (
        P("dp", ("context", "tensor"), None),
        P("dp", ("context", "tensor"), None),
        P("dp", None),
        P(None, "tensor"),
        P(None, None, "tensor"),
        P("tensor", None),
        P(),
        P(None, "tensor"),
        P(None, None, "tensor"),
        P(None, "tensor"),
        P(),
    )
    out_specs = (
        P("dp", ("context", "tensor"), None),
        P(),
        P(None, "tensor"),
        P(None, None, "tensor"),
        P(None, "tensor"),
        P(),
    )
    return jax.shard_map(local, mesh=mesh, in_specs=in_specs, out_specs=out_specs, check_vma=False)
```

profile of v0, /device:TPU:2, one launch (start us, length us, event | category | flops | bytes accessed | tf_op | source)
XLA Modules:
  0.0 926.9 jit_solution(11296037939888309069)
XLA Ops:
  10.3 1.8 multiply_cosine_fusion
  13.8 86.9 %all-gather.5.cloned.1.call-done = bf16[1,512,5376]{2,1,0:T(8,128)(2,1)} async-done(((bf16[1,32,5376]{2,1,0:T(8,128)(2,1)}), bf16[1,512,5376]{2,1,0:T(8,128)(2,1)}) %all-gather.5.cloned.1.call-update) | async-done | bytes 5505040 | tf_op jit(solution)/shard_map/all_gather | solution.py:121
  100.6 4.5 fusion.55
  105.2 3.5 fusion.15
  109.0 2.0 fusion.19
  112.5 2.0 collective-permute-start.1
  114.5 4.0 collective-permute-start
  121.4 1.9 copy.65
  123.3 2.0 copy.64
  125.3 67.7 %all-gather.7.cloned.1.call-done = bf16[1,512,5376]{2,1,0:T(8,128)(2,1)} async-done(((bf16[1,32,5376]{2,1,0:T(8,128)(2,1)}), bf16[1,512,5376]{2,1,0:T(8,128)(2,1)}) %all-gather.7.cloned.1.call-update) | async-done | bytes 5505040 | tf_op jit(solution)/shard_map/all_gather | solution.py:122
  193.0 4.2 fusion.61
  197.3 3.5 fusion.9
  205.6 2.2 fusion.75
  207.8 3.3 fusion.31
  211.1 2.8 fusion.22
  214.0 2.2 convolution_bitcast_fusion.1
  218.5 75.9 %psum.54 = bf16[512,16]{1,0:T(8,128)(2,1)} all-reduce(bf16[512,16]{1,0:T(8,128)(2,1)} %convolution_convert_fusion), channel_id=1, replica_groups=mesh['dp'=2,'context'=8,'tensor'=16] {'tensor'}, use_global_device_ids=true, to_apply=%region_7.8 | all-reduce | flops 8192 | bytes 32768 | tf_op jit(solution)/shard_map/psum | solution.py:269
  294.3 4.2 fusion
  305.7 1.8 copy.40
  308.6 6.3 collective-permute-done.3
  317.0 7.3 fusion.35
  325.1 5.6 fusion.38
  330.7 5.7 fusion.99
  336.4 14.6 %add_convert_fusion = bf16[512,5376]{1,0:T(8,128)(2,1)} fusion(f32[512,5376]{1,0:T(8,128)} %fusion.99, f32[512,5376]{1,0:T(8,128)} %fusion.35, f32[512,5376]{1,0:T(8,128)} %fusion.38, bf16[512,256]{0,1:T(8,128)(2,1)S(1)} %bitcast.198, bf16[5376,256]{1,0:T(8,128)(2,1)S(1)} %copy-done), kind=kOutput, calls=%fused_computation | convolution fusion | flops 1420296192 | bytes 41549824 | tf_op jit(solution)/shard_map/th,dh->td/dot_general | solution.py:284
  351.0 1.8 convolution_convert_fusion.1
  354.3 114.1 %all-reduce.10.cloned.1.call-done = bf16[16,5376]{1,0:T(8,128)(2,1)} async-done(((bf16[16,5376]{1,0:T(8,128)(2,1)}), bf16[16,5376]{1,0:T(8,128)(2,1)}) %all-reduce.10.cloned.1.call-update) | async-done | bytes 172048 | tf_op jit(solution)/shard_map/psum | solution.py:280
  472.0 90.5 %all-reduce.1 = (bf16[16,256]{1,0:T(8,128)(2,1)S(1)}, bf16[2,16,128]{2,1,0:T(8,128)(2,1)S(1)}, bf16[16,256]{1,0:T(8,128)(2,1)S(1)}) all-reduce(bf16[16,256]{1,0:T(8,128)(2,1)} %fusion.67, bf16[2,16,128]{2,1,0:T(8,128)(2,1)S(1)} %pad_maximum_fusion.12, ...), channel_id=1, replica_groups=mesh['dp'=2,'context'=8,'tensor'=16] {'dp','context'}, use_global_device_ids=true, to_apply=%region_4.5 | all-reduce | flops 12288 | bytes 49152 | tf_op jit(solution)/shard_map/psum | solution.py:275
  564.4 4.7 fusion.11
  569.1 85.8 %all-reduce.6.cloned.1.call-done = bf16[512,5376]{1,0:T(8,128)(2,1)} async-done(((bf16[512,5376]{1,0:T(8,128)(2,1)}), bf16[512,5376]{1,0:T(8,128)(2,1)}) %all-reduce.6.cloned.1.call-update) | async-done | bytes 5505040 | tf_op jit(solution)/shard_map/psum | solution.py:291
  654.9 1.7 fusion.77
  656.6 261.6 %all-reduce.8.cloned.1.call-done = f32[3,16,5376]{2,1,0:T(8,128)} async-done(((f32[3,16,5376]{2,1,0:T(8,128)}), f32[3,16,5376]{2,1,0:T(8,128)}) %all-reduce.8.cloned.1.call-update) | async-done | bytes 1032208 | tf_op jit(solution)/shard_map/psum | solution.py:273
  918.1 2.2 copy.69
  (122 shorter events, 34.3 us)
Async XLA Ops:
  7.2 111.4 %copy-start = (bf16[5376,256]{1,0:T(8,128)(2,1)S(1)}, bf16[5376,256]{1,0:T(8,128)(2,1)}, u32[]{:S(2)}) copy-start(bf16[5376,256]{1,0:T(8,128)(2,1)} %param.14) | copy-start | bytes 8257540
  7.2 93.5 %all-gather.5.cloned.1.call-start = ((), (), s32[]{:S(2)}) async-start(), calls=%async_computation.3 | async-start | bytes 5849088 | tf_op jit(solution)/shard_map/all_gather | solution.py:121
  7.9 185.1 %all-gather.7.cloned.1.call-start = ((), (), s32[]{:S(2)}) async-start(), calls=%async_computation.4 | async-start | bytes 5849088 | tf_op jit(solution)/shard_map/all_gather | solution.py:122
  8.7 459.8 %all-reduce.10.cloned.1.call-start = ((), (), s32[]{:S(2)}) async-start(), calls=%async_computation.2 | async-start | bytes 344064 | tf_op jit(solution)/shard_map/psum | solution.py:280
  8.7 102.4 %copy-start.32 = (f32[64]{0:T(128)}, f32[64]{0:T(128)S(1)}, u32[]{:S(2)}) copy-start(f32[64]{0:T(128)S(1)} %negate_power_fusion) | copy-start | bytes 772
  8.8 102.4 %copy-start.26 = (f32[512]{0:T(512)}, f32[512]{0:T(512)S(1)}, u32[]{:S(2)}) copy-start(f32[512]{0:T(512)S(1)} %fusion.114) | copy-start | bytes 6148
  100.6 4.5 copy-start.1
  105.2 15.1 %copy-start.20 = (bf16[512,48]{0,1:T(8,128)(2,1)}, bf16[512,48]{0,1:T(8,128)(2,1)S(1)}, u32[]{:S(2)}) copy-start(bf16[512,48]{0,1:T(8,128)(2,1)S(1)} %fusion.55) | copy-start | bytes 147460
  111.2 9.1 copy-start.29
  112.5 88.8 %collective-permute-start.1 = (bf16[2,512,1,128]{1,3,2,0:T(8,128)(2,1)}, bf16[2,512,1,128]{1,3,2,0:T(8,128)(2,1)}, u32[]{:S(2)}, u32[]{:S(2)}) collective-permute-start(bf16[2,512,1,128]{1,3,2,0:T(8,128)(2,1)} %pad_maximum_fusion.1), channel_id=1, source_target_pairs={{0,16},{16,32},{32,48},{48,64},{64,80},{80,96},{96,112},{1,17},{17... | collective-permute-start | bytes 786440 | tf_op jit(solution)/shard_map/ppermute | solution.py:16
  114.5 86.8 %collective-permute-start = (bf16[2,512,1,128]{1,3,2,0:T(8,128)(2,1)}, bf16[2,512,1,128]{1,3,2,0:T(8,128)(2,1)}, u32[]{:S(2)}, u32[]{:S(2)}) collective-permute-start(bf16[2,512,1,128]{1,3,2,0:T(8,128)(2,1)} %pad_maximum_fusion.1), channel_id=1, source_target_pairs={{0,32},{16,48},{32,64},{48,80},{64,96},{80,112},{1,33},{17,49},{33... | collective-permute-start | bytes 786440 | tf_op jit(solution)/shard_map/ppermute | solution.py:16
  193.0 4.2 copy-start.2
  197.3 4.0 copy-start.14
  197.3 4.0 copy-start.17
  197.3 4.0 copy-start.19
  207.8 9.7 %copy-start.15 = (bf16[128,2,512]{2,0,1:T(8,128)(2,1)}, bf16[128,2,512]{2,0,1:T(8,128)(2,1)S(1)}, u32[]{:S(2)}) copy-start(bf16[128,2,512]{2,0,1:T(8,128)(2,1)S(1)} %get-tuple-element.26) | copy-start | bytes 786436
  298.5 356.3 %all-reduce.6.cloned.1.call-start = ((), (), s32[]{:S(2)}) async-start(), calls=%async_computation | async-start | bytes 11010048 | tf_op jit(solution)/shard_map/psum | solution.py:291
  302.2 6.4 collective-permute-start.2
  303.5 11.3 %collective-permute-start.3 = (bf16[2,512,1,128]{1,3,2,0:T(8,128)(2,1)}, bf16[2,512,1,128]{1,3,2,0:T(8,128)(2,1)}, u32[]{:S(2)}, u32[]{:S(2)}) collective-permute-start(bf16[2,512,1,128]{1,3,2,0:T(8,128)(2,1)} %get-tuple-element.14), channel_id=1, source_target_pairs={{32,0},{48,16},{64,32},{80,48},{96,64},{112,80},{33,1},{49,17},{65... | collective-permute-start | bytes 786440 | tf_op jit(solution)/shard_map/ppermute | solution.py:16
  316.1 8.2 copy-start.5
  316.9 13.8 %copy-start.23 = (bf16[512,16]{0,1:T(8,128)(2,1)}, bf16[512,16]{0,1:T(8,128)(2,1)S(1)}, u32[]{:S(2)}) copy-start(bf16[512,16]{0,1:T(8,128)(2,1)S(1)} %fusion.66) | copy-start | bytes 49156
  316.9 7.4 copy-start.27
  317.0 7.4 copy-start.33
  317.0 7.9 copy-start.31
  317.0 8.1 copy-start.4
  324.9 5.8 copy-start.21
  324.9 5.8 copy-start.22
  325.0 5.7 copy-start.25
  325.0 5.7 copy-start.12
  330.7 5.7 copy-start.7
  351.0 120.2 %copy-start.6 = (f32[2,512,1,128]{1,3,2,0:T(8,128)S(1)}, f32[2,512,1,128]{1,3,2,0:T(8,128)}, u32[]{:S(2)}) copy-start(f32[2,512,1,128]{1,3,2,0:T(8,128)} %copy-done.5) | copy-start | bytes 1572868
  351.0 567.1 %all-reduce.8.cloned.1.call-start = ((), (), s32[]{:S(2)}) async-start(), calls=%async_computation.1 | async-start | bytes 2064384 | tf_op jit(solution)/shard_map/psum | solution.py:273
  (11 other events, 39.4 us)
Sparse Core Ops, SparseCore 0:
  9.8 90.8 all-gather.4
  102.4 90.5 all-gather.6
  298.6 169.7 all-reduce.9
  471.0 183.8 all-reduce.5
  660.7 257.3 all-reduce.7
where the time goes:
time: 928 us; the launch traced here: 927 us
  waiting for transfers between devices  624 us (67%)
  blocking collectives  166 us (18%)
  matrix products  84.1 us (9%)
  other arithmetic  19 us (2%)
  between operations  14.4 us (2%)
  local copies, waits for them, and re-layouts  10.5 us (1%)
    psum x1, waiting for transfers between devices, local(): grad_down_qkv = lax.psum(grad_down_part, ('dp', 'context', 'tensor'))  262 us
    psum x1, waiting for transfers between devices, local(): lax.psum(output_up_gradient_piece.astype(jnp.bfloat16), ('dp', 'context'))  114 us
    psum x1, blocking collectives, local(): lax.psum(query_up_gradient_piece.astype(jnp.bfloat16), ('dp', 'context'))  90.5 us
    all_gather x1, waiting for transfers between devices, local(): lax.all_gather(tokens[0], 'tensor', axis=0, tiled=True)  86.9 us
    psum x1, waiting for transfers between devices, local(): lax.psum((term + jnp.dot(hidden_all, down_factors_all, preferred_element_...  85.8 us
    psum x1, blocking collectives, local(): factor_value = lax.psum(factor_part.astype(jnp.bfloat16), 'tensor')  75.9 us
    all_gather x1, waiting for transfers between devices, local(): lax.all_gather(output_gradient[0], 'tensor', axis=0, tiled=True)  67.7 us
  transfers between devices with their start and end apart: 9, of which 6 were waited for; matrix products, arithmetic and copies ran while one was open for 10% of the time, Pallas kernels for 0%

commit v1 on v0

--- a/solution.py
+++ b/solution.py
@@ -2,6 +2,7 @@
 import jax.numpy as jnp
 from jax import lax
 from jax.sharding import PartitionSpec as P
+from jax.lax import all_gather
 
 HEAD_SIZE = 128
 WINDOW = 1024
@@ -277,9 +278,10 @@
         ),
         lax.psum(grad_up_kv_part.astype(jnp.bfloat16), ("dp", "context")).astype(jnp.float32),
         lax.psum(grad_down_out_part.astype(jnp.bfloat16), ("dp", "context")).astype(jnp.float32),
-        lax.psum(output_up_gradient_piece.astype(jnp.bfloat16), ("dp", "context")).astype(
-            jnp.float32
-        ),
+        jnp.sum(
+            all_gather(output_up_gradient_piece.astype(jnp.bfloat16), axis_name=("dp", "context")),
+            axis=0,
+        ).astype(jnp.float32),
     )
     term = jnp.einsum("th,dh->td", query_gradient, query_weight, preferred_element_type=jnp.float32)
     term = term + jnp.einsum(

time: 928 us -> 813 us (0.88)
  waiting for transfers between devices: 624 us -> 507 us
    psum x1 -> x0, waiting for transfers between devices: 114 us -> none  [local(): lax.psum(output_up_gradient_piece.astype(jnp.bfloat16), ('dp', 'context'))]
  transfers between devices with their start and end apart: 9 -> 9, of which waited for: 6 -> 5; matrix products, arithmetic and copies ran while one was open for 10% -> 13% of each run, Pallas kernels for 0% -> 0%
where the time goes in v1:
time: 813 us; the launch traced here: 812 us
  waiting for transfers between devices  507 us (62%)
  blocking collectives  164 us (20%)
  matrix products  86.8 us (11%)
  other arithmetic  18.8 us (2%)
  between operations  14.5 us (2%)
  local copies, waits for them, and re-layouts  11.9 us (1%)
  starting transfers between devices  9.02 us (1%)
    psum x1, waiting for transfers between devices, local(): grad_down_qkv = lax.psum(grad_down_part, ('dp', 'context', 'tensor'))  261 us
    psum x1, blocking collectives, local(): lax.psum(query_up_gradient_piece.astype(jnp.bfloat16), ('dp', 'context'))  88.4 us
    all_gather x1, waiting for transfers between devices, local(): lax.all_gather(tokens[0], 'tensor', axis=0, tiled=True)  86.8 us
    psum x1, waiting for transfers between devices, local(): lax.psum((term + jnp.dot(hidden_all, down_factors_all, preferred_element_...  84.5 us
    psum x1, blocking collectives, local(): factor_value = lax.psum(factor_part.astype(jnp.bfloat16), 'tensor')  75.9 us
    all_gather x1, waiting for transfers between devices, local(): lax.all_gather(output_gradient[0], 'tensor', axis=0, tiled=True)  66.1 us
  transfers between devices with their start and end apart: 9, of which 5 were waited for; matrix products, arithmetic and copies ran while one was open for 13% of the time, Pallas kernels for 0%

profile of v1, /device:TPU:2, one launch (start us, length us, event | category | flops | bytes accessed | tf_op | source)
XLA Modules:
  0.0 812.1 jit_solution(6351807161466027711)
XLA Ops:
  10.3 1.8 multiply_cosine_fusion
  12.1 1.7 fusion.29
  13.8 86.8 %all-gather.7.cloned.1.call-done = bf16[1,512,5376]{2,1,0:T(8,128)(2,1)} async-done(((bf16[1,32,5376]{2,1,0:T(8,128)(2,1)}), bf16[1,512,5376]{2,1,0:T(8,128)(2,1)}) %all-gather.7.cloned.1.call-update) | async-done | bytes 5505040 | tf_op jit(solution)/shard_map/all_gather | solution.py:122
  100.6 4.5 fusion.55
  105.2 3.5 fusion.15
  109.0 2.0 fusion.19
  112.5 2.0 collective-permute-start.1
  114.5 4.0 collective-permute-start
  121.3 1.9 copy.65
  123.3 2.0 copy.64
  125.2 66.1 %all-gather.9.cloned.1.call-done = bf16[1,512,5376]{2,1,0:T(8,128)(2,1)} async-done(((bf16[1,32,5376]{2,1,0:T(8,128)(2,1)}), bf16[1,512,5376]{2,1,0:T(8,128)(2,1)}) %all-gather.9.cloned.1.call-update) | async-done | bytes 5505040 | tf_op jit(solution)/shard_map/all_gather | solution.py:123
  191.4 4.2 fusion.61
  195.7 3.5 fusion.9
  204.2 2.3 fusion.75
  208.1 75.9 %psum.47 = bf16[512,16]{1,0:T(8,128)(2,1)} all-reduce(bf16[512,16]{1,0:T(8,128)(2,1)} %convolution_convert_fusion), channel_id=1, replica_groups=mesh['dp'=2,'context'=8,'tensor'=16] {'tensor'}, use_global_device_ids=true, to_apply=%region_7.8 | all-reduce | flops 8192 | bytes 32768 | tf_op jit(solution)/shard_map/psum | solution.py:270
  284.0 4.2 fusion
  288.3 4.3 fusion.31
  292.6 5.0 fusion.22
  305.4 1.8 copy.40
  308.3 6.5 collective-permute-done.3
  319.7 7.0 fusion.99
  326.7 5.6 fusion.38
  332.3 5.7 fusion.35
  338.0 14.6 %add_convert_fusion = bf16[512,5376]{1,0:T(8,128)(2,1)} fusion(f32[512,5376]{1,0:T(8,128)} %fusion.99, f32[512,5376]{1,0:T(8,128)} %fusion.35, f32[512,5376]{1,0:T(8,128)} %fusion.38, bf16[512,256]{0,1:T(8,128)(2,1)S(1)} %bitcast.199, bf16[5376,256]{1,0:T(8,128)(2,1)S(1)} %copy-done), kind=kOutput, calls=%fused_computation | convolution fusion | flops 1420296192 | bytes 41549824 | tf_op jit(solution)/shard_map/th,dh->td/dot_general | solution.py:286
  352.6 1.8 convolution_convert_fusion.1
  357.8 88.4 %all-reduce.1 = (bf16[16,256]{1,0:T(8,128)(2,1)S(1)}, bf16[2,16,128]{2,1,0:T(8,128)(2,1)S(1)}, bf16[16,256]{1,0:T(8,128)(2,1)S(1)}) all-reduce(bf16[16,256]{1,0:T(8,128)(2,1)} %fusion.67, bf16[2,16,128]{2,1,0:T(8,128)(2,1)S(1)} %pad_maximum_fusion.12, ...), channel_id=1, replica_groups=mesh['dp'=2,'context'=8,'tensor'=16] {'dp','context'}, use_global_device_ids=true, to_apply=%region_4.5 | all-reduce | flops 12288 | bytes 49152 | tf_op jit(solution)/shard_map/psum | solution.py:276
  448.0 4.7 fusion.11
  452.8 2.2 reduce_sum.22
  455.7 84.5 %all-reduce.5.cloned.1.call-done = bf16[512,5376]{1,0:T(8,128)(2,1)} async-done(((bf16[512,5376]{1,0:T(8,128)(2,1)}), bf16[512,5376]{1,0:T(8,128)(2,1)}) %all-reduce.5.cloned.1.call-update) | async-done | bytes 5505040 | tf_op jit(solution)/shard_map/psum | solution.py:293
  540.2 1.7 fusion.77
  541.9 261.4 %all-reduce.7.cloned.1.call-done = f32[3,16,5376]{2,1,0:T(8,128)} async-done(((f32[3,16,5376]{2,1,0:T(8,128)}), f32[3,16,5376]{2,1,0:T(8,128)}) %all-reduce.7.cloned.1.call-update) | async-done | bytes 1032208 | tf_op jit(solution)/shard_map/psum | solution.py:274
  803.3 2.2 copy.68
  (139 shorter events, 33.8 us)
Async XLA Ops:
  7.2 111.4 %copy-start = (bf16[5376,256]{1,0:T(8,128)(2,1)S(1)}, bf16[5376,256]{1,0:T(8,128)(2,1)}, u32[]{:S(2)}) copy-start(bf16[5376,256]{1,0:T(8,128)(2,1)} %param.14) | copy-start | bytes 8257540
  7.2 93.5 %all-gather.7.cloned.1.call-start = ((), (), s32[]{:S(2)}) async-start(), calls=%async_computation.2 | async-start | bytes 5849088 | tf_op jit(solution)/shard_map/all_gather | solution.py:122
  7.9 183.5 %all-gather.9.cloned.1.call-start = ((), (), s32[]{:S(2)}) async-start(), calls=%async_computation.3 | async-start | bytes 5849088 | tf_op jit(solution)/shard_map/all_gather | solution.py:123
  8.7 444.1 %all-gather.11.cloned.1.call-start = ((), (), s32[]{:S(2)}) async-start(), calls=%async_computation.4 | async-start | bytes 2924544 | tf_op jit(solution)/shard_map/all_gather | solution.py:282
  8.7 102.4 %copy-start.41 = (f32[64]{0:T(128)}, f32[64]{0:T(128)S(1)}, u32[]{:S(2)}) copy-start(f32[64]{0:T(128)S(1)} %negate_power_fusion) | copy-start | bytes 772
  8.8 102.4 %copy-start.37 = (f32[512]{0:T(512)}, f32[512]{0:T(512)S(1)}, u32[]{:S(2)}) copy-start(f32[512]{0:T(512)S(1)} %fusion.114) | copy-start | bytes 6148
  100.6 4.5 copy-start.1
  105.2 15.0 %copy-start.29 = (bf16[512,48]{0,1:T(8,128)(2,1)}, bf16[512,48]{0,1:T(8,128)(2,1)S(1)}, u32[]{:S(2)}) copy-start(bf16[512,48]{0,1:T(8,128)(2,1)S(1)} %fusion.55) | copy-start | bytes 147460
  111.2 9.1 %copy-start.39 = (bf16[16,256]{1,0:T(8,128)(2,1)S(1)}, bf16[16,256]{1,0:T(8,128)(2,1)}, u32[]{:S(2)}) copy-start(bf16[16,256]{1,0:T(8,128)(2,1)} %param.18) | copy-start | bytes 24580
  112.5 87.2 %collective-permute-start.1 = (bf16[2,512,1,128]{1,3,2,0:T(8,128)(2,1)}, bf16[2,512,1,128]{1,3,2,0:T(8,128)(2,1)}, u32[]{:S(2)}, u32[]{:S(2)}) collective-permute-start(bf16[2,512,1,128]{1,3,2,0:T(8,128)(2,1)} %pad_maximum_fusion.1), channel_id=1, source_target_pairs={{0,16},{16,32},{32,48},{48,64},{64,80},{80,96},{96,112},{1,17},{17... | collective-permute-start | bytes 786440 | tf_op jit(solution)/shard_map/ppermute | solution.py:17
  114.5 85.2 %collective-permute-start = (bf16[2,512,1,128]{1,3,2,0:T(8,128)(2,1)}, bf16[2,512,1,128]{1,3,2,0:T(8,128)(2,1)}, u32[]{:S(2)}, u32[]{:S(2)}) collective-permute-start(bf16[2,512,1,128]{1,3,2,0:T(8,128)(2,1)} %pad_maximum_fusion.1), channel_id=1, source_target_pairs={{0,32},{16,48},{32,64},{48,80},{64,96},{80,112},{1,33},{17,49},{33... | collective-permute-start | bytes 786440 | tf_op jit(solution)/shard_map/ppermute | solution.py:17
  191.4 4.2 copy-start.2
  195.7 4.1 copy-start.19
  195.7 4.1 copy-start.26
  199.5 4.7 copy-start.32
  288.2 251.9 %all-reduce.5.cloned.1.call-start = ((), (), s32[]{:S(2)}) async-start(), calls=%async_computation | async-start | bytes 11010048 | tf_op jit(solution)/shard_map/psum | solution.py:293
  288.3 4.3 copy-start.17
  288.3 4.3 copy-start.33
  292.6 6.5 copy-start.9
  292.6 5.0 copy-start.22
  292.6 5.0 copy-start.24
  297.6 6.6 copy-start.11
  297.6 6.6 copy-start.13
  300.0 8.3 %collective-permute-start.2 = (bf16[2,512,1,128]{1,3,2,0:T(8,128)(2,1)}, bf16[2,512,1,128]{1,3,2,0:T(8,128)(2,1)}, u32[]{:S(2)}, u32[]{:S(2)}) collective-permute-start(bf16[2,512,1,128]{1,3,2,0:T(8,128)(2,1)} %get-tuple-element.13), channel_id=1, source_target_pairs={{16,0},{32,16},{48,32},{64,48},{80,64},{96,80},{112,96},{17,1},{33... | collective-permute-start | bytes 786440 | tf_op jit(solution)/shard_map/ppermute | solution.py:17
  301.3 13.5 %collective-permute-start.3 = (bf16[2,512,1,128]{1,3,2,0:T(8,128)(2,1)}, bf16[2,512,1,128]{1,3,2,0:T(8,128)(2,1)}, u32[]{:S(2)}, u32[]{:S(2)}) collective-permute-start(bf16[2,512,1,128]{1,3,2,0:T(8,128)(2,1)} %get-tuple-element.14), channel_id=1, source_target_pairs={{32,0},{48,16},{64,32},{80,48},{96,64},{112,80},{33,1},{49,17},{65... | collective-permute-start | bytes 786440 | tf_op jit(solution)/shard_map/ppermute | solution.py:17
  316.0 16.4 %copy-start.6 = (f32[2,512,1,128]{1,3,2,0:T(8,128)}, f32[2,512,1,128]{1,3,2,0:T(8,128)S(1)}, u32[]{:S(2)}) copy-start(f32[2,512,1,128]{1,3,2,0:T(8,128)S(1)} %fusion.74) | copy-start | bytes 1572868
  317.3 9.3 %copy-start.30 = (bf16[512,1,64]{0,2,1:T(8,128)(2,1)}, bf16[512,1,64]{0,2,1:T(8,128)(2,1)S(1)}, u32[]{:S(2)}) copy-start(bf16[512,1,64]{0,2,1:T(8,128)(2,1)S(1)} %get-tuple-element.17) | copy-start | bytes 196612
  317.4 9.3 %copy-start.31 = (bf16[512,1,64]{0,2,1:T(8,128)(2,1)}, bf16[512,1,64]{0,2,1:T(8,128)(2,1)S(1)}, u32[]{:S(2)}) copy-start(bf16[512,1,64]{0,2,1:T(8,128)(2,1)S(1)} %get-tuple-element.18) | copy-start | bytes 196612
  319.7 7.0 copy-start.4
  332.3 5.7 copy-start.8
  352.6 4.4 copy-start.7
  352.6 450.8 %all-reduce.7.cloned.1.call-start = ((), (), s32[]{:S(2)}) async-start(), calls=%async_computation.1 | async-start | bytes 2064384 | tf_op jit(solution)/shard_map/psum | solution.py:274
  (19 other events, 56.9 us)
Sparse Core Ops, SparseCore 0:
  9.8 90.8 all-gather.6
  102.4 88.9 all-gather.8
  288.4 69.6 all-gather.10
  360.5 179.5 all-reduce.4
  546.1 257.2 all-reduce.6
